TPU v7x, 128 devices: a whole 4x4x4 slice. The times are simulated.
128 devices in a mesh: grp: 8 (over x, z_hi), fac: 16 (over y, z_lo, core).
Axes of the slice: x: 4, y: 4, z: 4 (z_hi: 2, z_lo: 2; z = z_hi * 2 + z_lo), core: 2. Of those that a mesh axis runs over, the one named last changes fastest.
Arguments:
- metric_panels: bfloat16 [32768, 2048], P('fac'), may hold values from -0.1875 to 0.1875
- diag_inverses: float32 [2, 1024, 1024], replicated, as said below
- pair_batch: bfloat16 [32768, 8192], P('fac', 'grp'), may hold values from -6 to 6
Outputs:
- solved: bfloat16 [32768, 8192], P('fac', 'grp')
Inputs may be any that keep to these rules, and one draw needn't show every extreme that they name: `diag_inverses`: each of the two blocks is lower triangular with a positive diagonal.
All inputs are finite; a program needn't handle non-finite values.
Results may differ from a plain program's by a relative error of at most 0.006.
Values may be sent and summed in bfloat16 or wider, within the bound.
No kernel may reach another device: no remote copies, remote signals or barrier semaphores. Data moves between devices by JAX's collectives and lax.ppermute only.
A program may use at most 128 MiB of HBM per device.

v0:
```python
import jax
import jax.numpy as jnp
from jax import lax
from jax.sharding import PartitionSpec as P


def spread(value, axis, source):
    kept = jnp.where(lax.axis_index(axis) == source, value, 0).astype(value.dtype)
    return lax.psum(kept, axis)


def times_transposed(left, right):
    return lax.dot_general(
        left,
        right,
        (((1,), (1,)), ((), ())),
        precision=lax.Precision.HIGHEST,
        preferred_element_type=jnp.float32,
    )


def product(left, right):
    return jnp.dot(left, right, precision=lax.Precision.HIGHEST, preferred_element_type=jnp.float32)


def gather_factor(piece):
    return lax.all_gather(piece, "grp", axis=0, tiled=True)


def body(metric_panels, diag_inverses, pair_batch):
    panel_size = diag_inverses.shape[1]
    pair_count = pair_batch.shape[1]
    local_rows = pair_batch.shape[0]
    first_inverse = diag_inverses[0]
    second_inverse = diag_inverses[1]
    fac_index = lax.axis_index("fac")
    empty = jnp.zeros((panel_size, pair_count), jnp.float32)
    share_rows = local_rows // lax.axis_size("grp")
    row_start = lax.axis_index("grp") * share_rows
    own_metric = lax.dynamic_slice_in_dim(metric_panels, row_start, share_rows, 0).astype(
        jnp.float32
    )
    first_share = times_transposed(own_metric[:, :panel_size], first_inverse)
    factor_first = gather_factor(first_share)
    cross_rows = spread(factor_first[panel_size : 2 * panel_size], "fac", 0)
    updated = own_metric[:, panel_size:] - times_transposed(first_share, cross_rows)
    factor_second = gather_factor(times_transposed(updated, second_inverse))

    def solve_first(upper):
        return product(first_inverse, upper.astype(jnp.float32))

    def solve_second(lower, first_solved):
        return product(
            second_inverse, lower.astype(jnp.float32) - product(cross_rows, first_solved)
        )

    def chained_rest(first_solved, second_solved):
        partial_rest = pair_batch.astype(jnp.float32) - product(factor_first, first_solved)
        return partial_rest - product(factor_second, second_solved)

    first_local = lax.cond(
        fac_index == 0, lambda: solve_first(pair_batch[:panel_size]), lambda: empty
    )
    first_solved = spread(first_local, "fac", 0)
    second_local = lax.cond(
        fac_index == 0,
        lambda: solve_second(pair_batch[panel_size : 2 * panel_size], first_solved),
        lambda: empty,
    )
    second_solved = spread(second_local.astype(jnp.bfloat16), "fac", 0).astype(second_local.dtype)
    result = lax.cond(
        fac_index == 0,
        lambda: jnp.concatenate([first_solved, second_solved], axis=0),
        lambda: chained_rest(first_solved, second_solved),
    )
    return result.astype(jnp.bfloat16)


def solution(mesh):
    in_specs = (P("fac", None), P(), P("fac", "grp"))
    out_specs = P("fac", "grp")
    return jax.shard_map(body, mesh=mesh, in_specs=in_specs, out_specs=out_specs, check_vma=False)
```

profile of v0, /device:TPU:1, one launch (start us, length us, event | category | flops | bytes accessed | tf_op | source)
XLA Modules:
  0.0 670.5 jit_solution(1340951626374905802)
XLA Ops:
  6.5 5.5 fusion.8
  12.0 0.0 all-gather.3.cloned.1.call-update
  12.1 0.0 all-reduce.6.cloned.1.call-start
  12.1 8.5 %slice_bitcast_fusion = (f32[1024,1024]{1,0:T(8,128)}, f32[1024,1024]{1,0:T(8,128)}) fusion(f32[2,1024,1024]{2,1,0:T(8,128)} %param.10), kind=kLoop, calls=%fused_computation.10 | loop fusion | bytes 16777216 | tf_op jit(solution)/shard_map/squeeze | solution.py:35
  20.6 2.5 conditional.8
  20.6 2.5 broadcast_in_dim.11
  23.1 2.8 broadcast_select_fusion
  25.8 97.3 %all-gather.3.cloned.1.call-done = f32[2048,1024]{1,0:T(8,128)} async-done(((f32[256,1024]{1,0:T(8,128)}), f32[2048,1024]{1,0:T(8,128)}) %all-gather.3.cloned.1.call-update) | async-done | bytes 8388624 | tf_op jit(solution)/shard_map/all_gather | solution.py:27
  123.1 5.0 slice_select_fusion
  128.2 0.0 all-reduce.4.cloned.1.call-start
  128.2 194.1 %all-reduce.6.cloned.1.call-done = (f32[1024,1024]{1,0:T(8,128)}, f32[1024,1024]{1,0:T(8,128)}) async-done(((f32[1024,1024]{1,0:T(8,128)}, f32[1024,1024]{1,0:T(8,128)}), (f32[1024,1024]{1,0:T(8,128)}, f32[1024,1024]{1,0:T(8,128)})) %all-reduce.6.cloned.1.call-update) | async-done | bytes 8388624 | tf_op jit(solution)/shard_map/psum | solution.py:9
  322.3 6.5 conditional.9
  322.3 0.3 broadcast_in_dim.12.clone
  328.8 1.5 broadcast_select_fusion.1
  330.3 0.0 all-gather.5.cloned.1.call-start
  330.3 0.1 copy-done.1
  330.4 6.0 convolution_subtract_fusion
  336.4 6.9 %fusion.11 = f32[256,1024]{1,0:T(8,128)} fusion(f32[256,1024]{1,0:T(8,128)S(1)} %convolution_subtract_fusion, f32[2,1024,1024]{2,1,0:T(8,128)} %param.10), kind=kOutput, calls=%fused_computation.18 | convolution fusion | flops 3221225472 | bytes 6291456 | tf_op jit(solution)/shard_map/dot_general | solution.py:13
  343.3 148.5 %all-reduce.4.cloned.1.call-done = bf16[1024,1024]{1,0:T(8,128)(2,1)} async-done(((bf16[1024,1024]{1,0:T(8,128)(2,1)}), bf16[1024,1024]{1,0:T(8,128)(2,1)}) %all-reduce.4.cloned.1.call-update) | async-done | bytes 2097168 | tf_op jit(solution)/shard_map/psum | solution.py:9
  491.8 4.1 convert_element_type.40
  495.9 107.0 %all-gather.5.cloned.1.call-done = f32[2048,1024]{1,0:T(8,128)} async-done(((f32[256,1024]{1,0:T(8,128)}), f32[2048,1024]{1,0:T(8,128)}) %all-gather.5.cloned.1.call-update) | async-done | bytes 8388624 | tf_op jit(solution)/shard_map/all_gather | solution.py:27
  602.9 60.8 %conditional.10 = (bf16[2048,1024]{1,0:T(8,128)(2,1)}) conditional(s32[]{:T(128)} %convert_element_type.39, (bf16[2048,1024]{1,0:T(8,128)(2,1)}, f32[2048,1024]{1,0:T(8,128)}, f32[1024,1024]{1,0:T(8,128)}, f32[2048,1024]{1,0:T(8,128)}, f32[1024,1024]{1,0:T(8,128)}) %tuple.39, (f32[1024,1024]{1,0:T(8,128)}, f32[1024,1024]{1,0:T(8,128)}) %tuple.40), branch_computations={%region_7.8_spmd, %region_8.9_spmd} | conditional | flops 51547996160 | bytes 117440608
  603.1 31.1 %fusion.13 = f32[2048,1024]{1,0:T(8,128)S(1)} fusion(f32[2048,1024]{1,0:T(8,128)} %get-tuple-element.54, f32[1024,1024]{1,0:T(8,128)} %get-tuple-element.55), kind=kOutput, calls=%fused_computation.20 | convolution fusion | flops 25769803776 | bytes 20971520 | tf_op jit(solution)/shard_map/cond/branch_0_fun/dot_general | solution.py:23
  634.2 29.3 %subtract_subtract_fusion = bf16[2048,1024]{1,0:T(8,128)(2,1)} fusion(f32[2048,1024]{1,0:T(8,128)S(1)} %fusion.13, bf16[2048,1024]{1,0:T(8,128)(2,1)S(1)} %copy-done.5, f32[2048,1024]{1,0:T(8,128)S(1)} %copy-done.3, f32[1024,1024]{1,0:T(8,128)S(1)} %copy-done), kind=kOutput, calls=%fused_computation.7 | convolution fusion | flops 25778192384 | bytes 29360128 | tf_op jit(solution)/shard_map/cond/branch_0_fun/dot_general | solution.py:23
  (11 shorter events, 0.1 us)
Async XLA Ops:
  6.5 116.6 %all-gather.3.cloned.1.call-start = ((), (), s32[]{:S(2)}) async-start(), calls=%async_computation | async-start | bytes 9437184 | tf_op jit(solution)/shard_map/all_gather | solution.py:27
  12.1 310.3 %all-reduce.6.cloned.1.call-start = ((), (), s32[]{:S(2)}) async-start(), calls=%async_computation.3 | async-start | bytes 16777216 | tf_op jit(solution)/shard_map/psum | solution.py:9
  128.2 363.7 %all-reduce.4.cloned.1.call-start = ((), (), s32[]{:S(2)}) async-start(), calls=%async_computation.2 | async-start | bytes 4194304 | tf_op jit(solution)/shard_map/psum | solution.py:9
  328.8 1.6 copy-start.1
  330.3 272.6 %all-gather.5.cloned.1.call-start = ((), (), s32[]{:S(2)}) async-start(), calls=%async_computation.1 | async-start | bytes 9437184 | tf_op jit(solution)/shard_map/all_gather | solution.py:27
  603.1 31.1 %copy-start = (f32[1024,1024]{1,0:T(8,128)S(1)}, f32[1024,1024]{1,0:T(8,128)}, u32[]{:S(2)}) copy-start(f32[1024,1024]{1,0:T(8,128)} %get-tuple-element.57) | copy-start | bytes 12582916 | tf_op jit(solution)/shard_map/conditional.1
  603.1 31.1 %copy-start.3 = (f32[2048,1024]{1,0:T(8,128)S(1)}, f32[2048,1024]{1,0:T(8,128)}, u32[]{:S(2)}) copy-start(f32[2048,1024]{1,0:T(8,128)} %get-tuple-element.56) | copy-start | bytes 25165828 | tf_op jit(solution)/shard_map/conditional.1
  603.1 31.1 %copy-start.5 = (bf16[2048,1024]{1,0:T(8,128)(2,1)S(1)}, bf16[2048,1024]{1,0:T(8,128)(2,1)}, u32[]{:S(2)}) copy-start(bf16[2048,1024]{1,0:T(8,128)(2,1)} %get-tuple-element.53) | copy-start | bytes 12582916 | tf_op jit(solution)/shard_map/conditional.1
Sparse Core Ops, SparseCore 0:
  12.2 110.8 all-gather.2
  128.3 193.9 all-reduce.5
  330.4 161.3 all-reduce.3
  494.0 108.8 all-gather.4
where the time goes:
time: 677 us; the launch traced here: 670 us
  waiting for transfers between devices  547 us (81%)
  matrix products  78.7 us (12%)
  between operations  13.4 us (2%)
  other arithmetic  13.3 us (2%)
  local copies, waits for them, and re-layouts  11.3 us (2%)
    psum x2, waiting for transfers between devices, spread(): return lax.psum(kept, axis)  343 us
    all_gather x2, waiting for transfers between devices, gather_factor(): return lax.all_gather(piece, 'grp', axis=0, tiled=True)  204 us
    dot_general x2, matrix products, product(): jnp.dot(left, right, precision=lax.Precision.HIGHEST, preferred_element_t...  60.3 us
    dot_general x3, matrix products, times_transposed(): lax.dot_general(left, right, (((1,), (1,)), ((), ())), precision=lax.Prec...  18.4 us
  transfers between devices with their start and end apart: 4, of which 4 were waited for; matrix products, arithmetic and copies ran while one was open for 5% of the time, Pallas kernels for 0%

commit v1 on v0

--- a/solution.py
+++ b/solution.py
@@ -2,6 +2,11 @@
 import jax.numpy as jnp
 from jax import lax
 from jax.sharding import PartitionSpec as P
+
+
+def gather_over(block, name, along):
+    sent = jnp.stack([block] * lax.axis_size(name))
+    return jnp.concatenate(lax.all_to_all(sent, name, 0, 0), axis=along)
 
 
 def spread(value, axis, source):
@@ -24,7 +29,7 @@
 
 
 def gather_factor(piece):
-    return lax.all_gather(piece, "grp", axis=0, tiled=True)
+    return gather_over(piece, "grp", 0)
 
 
 def body(metric_panels, diag_inverses, pair_batch):

time: 677 us -> 637 us (0.941)
  waiting for transfers between devices: 547 us -> 498 us
  starting transfers between devices: 0.13 us -> 13.9 us
  local copies, waits for them, and re-layouts: 11.3 us -> 19.8 us
    all_gather x2 -> x0, waiting for transfers between devices: 204 us -> none  [gather_factor(): return lax.all_gather(piece, 'grp', axis=0, tiled=True)]
    all_to_all x0 -> x2, waiting for transfers between devices: none -> 101 us  [gather_over(): return jnp.concatenate(lax.all_to_all(sent, name, 0, 0), axis=along)]
    psum x2, waiting for transfers between devices: 343 us -> 396 us  [spread(): return lax.psum(kept, axis)]
    all_to_all x0 -> x2, starting transfers between devices: none -> 13.9 us  [gather_over(): return jnp.concatenate(lax.all_to_all(sent, name, 0, 0), axis=along)]
    another operation x6, local copies, waits for them, and re-layouts: 0.01 us -> 8.61 us  [the longest x2 8.6 us: gather_over(): sent = jnp.stack([block] * lax.axis_size(name))]
  transfers between devices with their start and end apart: 4 -> 4, of which waited for: 4 -> 3; matrix products, arithmetic and copies ran while one was open for 5% -> 3% of each run, Pallas kernels for 0% -> 0%
where the time goes in v1:
time: 637 us
  waiting for transfers between devices  498 us (78%)
  matrix products  78.6 us (12%)
  local copies, waits for them, and re-layouts  19.8 us (3%)
  starting transfers between devices  13.9 us (2%)
  between operations  13.5 us (2%)
  other arithmetic  13.2 us (2%)
    psum x2, waiting for transfers between devices, spread(): return lax.psum(kept, axis)  396 us
    all_to_all x2, waiting for transfers between devices, gather_over(): return jnp.concatenate(lax.all_to_all(sent, name, 0, 0), axis=along)  101 us
    dot_general x2, matrix products, product(): jnp.dot(left, right, precision=lax.Precision.HIGHEST, preferred_element_t...  62.3 us
    dot_general x3, matrix products, times_transposed(): lax.dot_general(left, right, (((1,), (1,)), ((), ())), precision=lax.Prec...  16.3 us
    all_to_all x2, starting transfers between devices, gather_over(): return jnp.concatenate(lax.all_to_all(sent, name, 0, 0), axis=along)  13.9 us
  transfers between devices with their start and end apart: 4, of which 3 were waited for; matrix products, arithmetic and copies ran while one was open for 3% of the time, Pallas kernels for 0%

profile of v1, /device:TPU:1, one launch (start us, length us, event | category | flops | bytes accessed | tf_op | source)
XLA Modules:
  0.0 636.9 jit_solution(11102831689402082281)
XLA Ops:
  6.5 4.5 fusion.8
  11.1 4.3 stack.4
  15.4 8.2 %all-to-all-start = ((f32[8,256,1024]{2,1,0:T(8,128)}), f32[8,256,1024]{2,1,0:T(8,128)}, u32[]{:S(2)}, u32[]{:S(2)}) async-start(f32[8,256,1024]{2,1,0:T(8,128)} %stack.4), calls=%async_computation | async-start | bytes 16777216 | tf_op jit(solution)/shard_map/all_to_all | solution.py:9
  23.5 0.0 all-reduce.6.cloned.1.call-start
  23.6 8.5 %slice_bitcast_fusion = (f32[1024,1024]{1,0:T(8,128)}, f32[1024,1024]{1,0:T(8,128)}) fusion(f32[2,1024,1024]{2,1,0:T(8,128)} %param.10), kind=kLoop, calls=%fused_computation.10 | loop fusion | bytes 16777216 | tf_op jit(solution)/shard_map/squeeze | solution.py:40
  32.0 2.5 conditional.8
  32.0 2.5 broadcast_in_dim.12
  34.6 2.8 broadcast_select_fusion
  37.3 101.4 %all-to-all-done = f32[8,256,1024]{2,1,0:T(8,128)} async-done(((f32[8,256,1024]{2,1,0:T(8,128)}), f32[8,256,1024]{2,1,0:T(8,128)}, u32[]{:S(2)}, u32[]{:S(2)}) %all-to-all-start) | async-done | bytes 8388640 | tf_op jit(solution)/shard_map/all_to_all | solution.py:9
  138.7 5.0 slice_select_fusion
  143.7 196.5 %all-reduce.6.cloned.1.call-done = (f32[1024,1024]{1,0:T(8,128)}, f32[1024,1024]{1,0:T(8,128)}) async-done(((f32[1024,1024]{1,0:T(8,128)}, f32[1024,1024]{1,0:T(8,128)}), (f32[1024,1024]{1,0:T(8,128)}, f32[1024,1024]{1,0:T(8,128)})) %all-reduce.6.cloned.1.call-update) | async-done | bytes 8388624 | tf_op jit(solution)/shard_map/psum | solution.py:14
  340.2 6.0 convolution_subtract_fusion
  346.2 5.7 fusion.11
  352.0 4.3 stack.5
  356.3 5.7 all-to-all-start.1
  362.0 0.0 all-reduce.4.cloned.1.call-start
  362.0 0.5 conditional.9
  362.0 0.3 broadcast_in_dim.13.clone
  362.6 1.5 broadcast_select_fusion.1
  364.0 199.7 %all-reduce.4.cloned.1.call-done = bf16[1024,1024]{1,0:T(8,128)(2,1)} async-done(((bf16[1024,1024]{1,0:T(8,128)(2,1)}), bf16[1024,1024]{1,0:T(8,128)(2,1)}) %all-reduce.4.cloned.1.call-update) | async-done | bytes 2097168 | tf_op jit(solution)/shard_map/psum | solution.py:14
  563.8 4.0 convert_element_type.40
  567.8 62.3 %conditional.10 = (bf16[2048,1024]{1,0:T(8,128)(2,1)}) conditional(s32[]{:T(128)} %convert_element_type.39, (bf16[2048,1024]{1,0:T(8,128)(2,1)}, f32[8,256,1024]{2,1,0:T(8,128)}, f32[1024,1024]{1,0:T(8,128)}, f32[8,256,1024]{2,1,0:T(8,128)}, f32[1024,1024]{1,0:T(8,128)}) %tuple.39, (f32[1024,1024]{1,0:T(8,128)}, f32[1024,1024]{1,0:T(8,128)}) %tuple.40), branch_computations={%region_7.8_spmd, %region_8.9_spmd} | conditional | flops 51547996160 | bytes 83886144
  567.8 31.1 %fusion.13 = f32[2048,1024]{1,0:T(8,128)S(1)} fusion(f32[2048,1024]{1,0:T(8,128)} %bitcast.1, f32[1024,1024]{1,0:T(8,128)} %get-tuple-element.55), kind=kOutput, calls=%fused_computation.20 | convolution fusion | flops 25769803776 | bytes 20971520 | tf_op jit(solution)/shard_map/cond/branch_0_fun/dot_general | solution.py:28
  598.8 31.3 %subtract_subtract_fusion = bf16[2048,1024]{1,0:T(8,128)(2,1)} fusion(f32[2048,1024]{1,0:T(8,128)S(1)} %fusion.13, bf16[2048,1024]{1,0:T(8,128)(2,1)S(1)} %copy-done.3, f32[2048,1024]{1,0:T(8,128)} %bitcast.2, f32[1024,1024]{1,0:T(8,128)S(1)} %copy-done), kind=kOutput, calls=%fused_computation.7 | convolution fusion | flops 25778192384 | bytes 29360128 | tf_op jit(solution)/shard_map/cond/branch_0_fun/dot_general | solution.py:28
  (7 shorter events, 0.0 us)
Async XLA Ops:
  15.4 123.3 %all-to-all-start = ((f32[8,256,1024]{2,1,0:T(8,128)}), f32[8,256,1024]{2,1,0:T(8,128)}, u32[]{:S(2)}, u32[]{:S(2)}) async-start(f32[8,256,1024]{2,1,0:T(8,128)} %stack.4), calls=%async_computation | async-start | bytes 16777216 | tf_op jit(solution)/shard_map/all_to_all | solution.py:9
  23.5 316.7 %all-reduce.6.cloned.1.call-start = ((), (), s32[]{:S(2)}) async-start(), calls=%async_computation.3 | async-start | bytes 16777216 | tf_op jit(solution)/shard_map/psum | solution.py:14
  356.3 211.5 %all-to-all-start.1 = ((f32[8,256,1024]{2,1,0:T(8,128)}), f32[8,256,1024]{2,1,0:T(8,128)}, u32[]{:S(2)}, u32[]{:S(2)}) async-start(f32[8,256,1024]{2,1,0:T(8,128)} %stack.5), calls=%async_computation.1 | async-start | bytes 16777216 | tf_op jit(solution)/shard_map/all_to_all | solution.py:9
  362.0 201.8 %all-reduce.4.cloned.1.call-start = ((), (), s32[]{:S(2)}) async-start(), calls=%async_computation.2 | async-start | bytes 4194304 | tf_op jit(solution)/shard_map/psum | solution.py:14
  567.8 31.1 %copy-start = (f32[1024,1024]{1,0:T(8,128)S(1)}, f32[1024,1024]{1,0:T(8,128)}, u32[]{:S(2)}) copy-start(f32[1024,1024]{1,0:T(8,128)} %get-tuple-element.57) | copy-start | bytes 12582916 | tf_op jit(solution)/shard_map/conditional.1
  567.8 31.1 %copy-start.3 = (bf16[2048,1024]{1,0:T(8,128)(2,1)S(1)}, bf16[2048,1024]{1,0:T(8,128)(2,1)}, u32[]{:S(2)}) copy-start(bf16[2048,1024]{1,0:T(8,128)(2,1)} %get-tuple-element.53) | copy-start | bytes 12582916 | tf_op jit(solution)/shard_map/conditional.1
Sparse Core Ops, SparseCore 0:
  143.8 196.2 all-reduce.5
  365.3 198.4 all-reduce.3
